TPU v7x, 512 devices: a whole 4x4x16 slice. The times are simulated.
512 devices in a mesh: row: 32 (over y, x, core), col: 16 (over z).
Axes of the slice: x: 4, y: 4, z: 16, core: 2. Of those that a mesh axis runs over, the one named last changes fastest.
Arguments:
- covariance: bfloat16 [16384, 16384], P('row', 'col'), as said below
- coef_index: int32 [3, 16384], replicated, may hold values from 0 to 127, as said below
Outputs:
- grid_cov: float32 [4608, 4608], P('row', 'col')
Inputs may be any that keep to these rules, and one draw needn't show every extreme that they name: `coef_index`: every (degree l, order m, parity c) with m <= l < 128, c in 0 and 1, and c = 0 where m = 0, names exactly one row. The rows of each order are consecutive: cosine terms by rising degree, then sine terms by rising degree. Orders m and 128 - m (0 and 64) stand next to each other, the smaller first, and fill 2 * 128 rows together; pairs start at multiples of 256. Columns follow the same index. `covariance`: Symmetric.
All inputs are finite; a program needn't handle non-finite values.
Results may differ from a plain program's by a relative error of at most 0.0028.
Values sent between devices are 32-bit elements; how exact they have to be, the bound alone decides.
A program may use at most 64 MiB of HBM per device.

v0:
```python
import math

import jax
import jax.numpy as jnp
from jax import lax
from jax.sharding import PartitionSpec as P

LL = 128
NLON = 384
NLAT = 12


def legendre_rows(lat_count, lon_count, degree_count):
    grid_rows = lon_count // 2
    first_row = grid_rows // 2 - lat_count // 2
    colatitude = (first_row + jnp.arange(lat_count, dtype=jnp.float32) + 0.5) * (
        math.pi / grid_rows
    )
    cosine = jnp.cos(colatitude)[:, None]
    sine_vals = jnp.sin(colatitude)[:, None]
    orders = jnp.arange(degree_count, dtype=jnp.float32)[None, :]
    growth = jnp.sqrt((2.0 * orders + 1.0) / jnp.maximum(2.0 * orders, 1.0))
    growth = jnp.where(
        orders == 1.0, jnp.sqrt(jnp.float32(3.0)), jnp.where(orders == 0.0, 1.0, growth)
    )
    sectoral = jnp.exp(jnp.cumsum(jnp.log(growth), axis=1) + orders * jnp.log(sine_vals))

    def advance(state_pair, degree):
        before, earlier = state_pair
        deg_sum = degree + orders
        deg_diff = degree - orders
        alpha_lm = jnp.sqrt(
            jnp.maximum((2.0 * degree - 1.0) * (2.0 * degree + 1.0), 0.0)
            / jnp.maximum(deg_diff * deg_sum, 1.0)
        )
        beta_lm = jnp.sqrt(
            jnp.maximum((2.0 * degree + 1.0) * (deg_sum - 1.0) * (deg_diff - 1.0), 0.0)
            / jnp.maximum(deg_diff * deg_sum * (2.0 * degree - 3.0), 1.0)
        )
        general = alpha_lm * cosine * before - beta_lm * earlier
        current = jnp.where(orders < degree, general, jnp.where(orders == degree, sectoral, 0.0))
        return ((current, before), current)

    start_pair = (
        jnp.zeros((lat_count, degree_count), jnp.float32),
        jnp.zeros((lat_count, degree_count), jnp.float32),
    )
    _, stacked = lax.scan(
        advance, start_pair, jnp.arange(degree_count, dtype=jnp.float32), unroll=16
    )
    return jnp.transpose(stacked, (1, 0, 2)).reshape(lat_count, degree_count * degree_count)


def fourier(modes, parity, longitudes):
    phases = longitudes[:, None] * modes[None, :] % NLON
    angles = phases.astype(jnp.float32) * (2.0 * math.pi / NLON)
    return jnp.where(parity[None, :] == 0, jnp.cos(angles), jnp.sin(angles))


def block_slots(orders_flat, blocks, length, slot_count):
    grouped = orders_flat.reshape(blocks, length)
    change = jnp.concatenate(
        [jnp.ones((blocks, 1), jnp.int32), (grouped[:, 1:] != grouped[:, :-1]).astype(jnp.int32)],
        axis=1,
    )
    slot_ids = jnp.cumsum(change, axis=1) - 1
    first_marks = (
        slot_ids[:, :, None] == jnp.arange(slot_count, dtype=jnp.int32)[None, None, :]
    ) & (change[:, :, None] == 1)
    firsts = jnp.sum(jnp.where(first_marks, grouped[:, :, None], 0), axis=1)
    return (slot_ids, firsts)


def spectral_weights(plm_table, degree, orders, parity, slot_ids, slot_count):
    values = plm_table[:, degree * LL + orders]
    key_ids = 2 * slot_ids + parity
    matches = key_ids[None, None, :] == jnp.arange(2 * slot_count, dtype=jnp.int32)[None, :, None]
    return jnp.where(matches, values[:, None, :], 0.0)


def on_device(covariance, coef_index):
    rows_dev, cols_dev = covariance.shape
    row_count = lax.axis_size("row")
    col_count = lax.axis_size("col")
    row_place = lax.axis_index("row")
    col_place = lax.axis_index("col")
    row_orders = max(LL // row_count, 2)
    col_orders = max(LL // col_count, 2)
    plm_table = legendre_rows(NLAT, NLON, LL)
    row_slots, row_firsts = block_slots(coef_index[1], row_count, rows_dev, row_orders)
    col_slots, col_firsts = block_slots(coef_index[1], col_count, cols_dev, col_orders)
    mine_rows = lax.dynamic_slice_in_dim(coef_index, row_place * rows_dev, rows_dev, 1)
    mine_cols = lax.dynamic_slice_in_dim(coef_index, col_place * cols_dev, cols_dev, 1)
    own_row_slots = lax.dynamic_index_in_dim(row_slots, row_place, 0, keepdims=False)
    own_col_slots = lax.dynamic_index_in_dim(col_slots, col_place, 0, keepdims=False)
    row_weights = spectral_weights(
        plm_table, mine_rows[0], mine_rows[1], mine_rows[2], own_row_slots, row_orders
    )
    row_weights = row_weights.astype(jnp.bfloat16).reshape(NLAT * 2 * row_orders, rows_dev)
    col_weights = spectral_weights(
        plm_table, mine_cols[0], mine_cols[1], mine_cols[2], own_col_slots, col_orders
    )
    first_pass = jnp.dot(row_weights, covariance, preferred_element_type=jnp.float32)
    second = jnp.einsum("ak,jbk->ajb", first_pass, col_weights, precision=lax.Precision.HIGHEST)
    width_cols = NLAT * 2 * col_orders
    second = second.reshape(NLAT, 2 * row_orders, width_cols)
    all_lons = jnp.arange(NLON, dtype=jnp.int32)
    row_modes = jnp.repeat(row_firsts.reshape(-1), 2)
    row_parity = jnp.arange(row_modes.shape[0], dtype=jnp.int32) % 2
    row_table = fourier(row_modes, row_parity, all_lons)
    grid_vals = jnp.einsum(
        "jq,iqc->jic",
        row_table,
        lax.all_to_all(second, "row", split_axis=2, concat_axis=1, tiled=True),
        precision=lax.Precision.HIGHEST,
    )
    row_done = lax.all_to_all(grid_vals, "row", split_axis=0, concat_axis=2, tiled=True)
    pts_row = row_done.shape[0] * NLAT
    spectral = row_done.reshape(pts_row, NLAT, 2 * col_orders)
    own_modes = jnp.repeat(lax.dynamic_index_in_dim(col_firsts, col_place, 0, keepdims=False), 2)
    own_parity = jnp.arange(2 * col_orders, dtype=jnp.int32) % 2
    pts_col = NLAT * NLON // col_count
    longitudes = jnp.arange(pts_col * lax.axis_size("col") // NLAT, dtype=jnp.int32)
    table_part = fourier(own_modes, own_parity, longitudes)
    grid_vals = jnp.einsum("jk,pik->jip", table_part, spectral, precision=lax.Precision.HIGHEST)
    summed = lax.psum_scatter(
        grid_vals.reshape(pts_col * lax.axis_size("col"), pts_row),
        "col",
        scatter_dimension=0,
        tiled=True,
    )
    result = summed.T
    return result


def solution(mesh):
    in_specs = (P("row", "col"), P())
    out_specs = P("row", "col")
    return jax.shard_map(
        on_device, mesh=mesh, in_specs=in_specs, out_specs=out_specs, check_vma=False
    )
```

profile of v0, /device:TPU:6, one launch (start us, length us, event | category | flops | bytes accessed | tf_op | source)
XLA Modules:
  0.0 453.2 jit_solution(14705494164497501560)
XLA Ops:
  6.7 1.2 fusion.291
  8.8 0.9 compare_select_fusion
  10.1 1.2 reduce-window.20
  12.5 4.5 reduce-window.30
  18.6 267.6 %while.19 = (s32[]{:T(128)}, f32[12,128]{1,0:T(8,128)S(1)}, f32[12,128]{1,0:T(8,128)S(1)}, f32[8,16,12,128]{3,2,1,0:T(8,128)S(1)}, f32[8,16]{1,0:T(8,128)S(1)}, ...) while((s32[]{:T(128)}, f32[12,128]{1,0:T(8,128)S(1)}, ...), condition=%wide.region_5.6_spmd.clone.clone, body=%wide.region_4.5_spmd.clone.clone.sunk | while | flops 359546 | bytes 878834 | solution.py:48
  286.1 4.7 %copy.75 = f32[128,12,128]{1,2,0:T(8,128)} copy(f32[128,12,128]{2,1,0:T(8,128)S(1)} %bitcast.392) | data formatting | bytes 1572864 | tf_op jit(solution)/shard_map/reshape | solution.py:48
  290.8 4.4 gather_fusion
  295.2 6.2 %gather_fusion.1 = f32[1024,12]{1,0:T(8,128)S(1)} fusion(f32[12,16384]{0,1:T(8,128)} %bitcast.387, s32[1024]{0:T(1024)S(1)} %broadcast_clamp_fusion), kind=kCustom, calls=%fused_computation.1 | custom fusion | bytes 102400 | tf_op jit(solution)/shard_map/gather | solution.py:75
  303.8 1.1 reshape.1773
  305.0 9.4 %all-to-all-start = ((f32[32,1,576]{2,1,0:T(1,128)}), f32[32,1,576]{2,1,0:T(1,128)S(1)}, u32[]{:S(2)}, u32[]{:S(2)}) async-start(f32[32,1,576]{2,1,0:T(1,128)} %reshape.1773), calls=%async_computation | async-start | bytes 163840 | tf_op jit(solution)/shard_map/all_to_all | solution.py:114
  315.6 4.7 %all-to-all-done = f32[32,1,576]{2,1,0:T(1,128)S(1)} async-done(((f32[32,1,576]{2,1,0:T(1,128)}), f32[32,1,576]{2,1,0:T(1,128)S(1)}, u32[]{:S(2)}, u32[]{:S(2)}) %all-to-all-start) | async-done | bytes 73760 | tf_op jit(solution)/shard_map/all_to_all | solution.py:114
  322.0 1.5 copy.89
  324.2 2.2 fusion.220
  327.0 1.4 reshape.1775
  328.4 5.5 %all-to-all-start.1 = ((f32[32,1,864]{2,1,0:T(1,128)}), f32[32,1,864]{2,1,0:T(1,128)S(1)}, u32[]{:S(2)}, u32[]{:S(2)}) async-start(f32[32,1,864]{2,1,0:T(1,128)} %reshape.1775), calls=%async_computation.1 | async-start | bytes 229376 | tf_op jit(solution)/shard_map/all_to_all | solution.py:117
  334.2 5.7 %all-to-all-done.1 = f32[32,1,864]{2,1,0:T(1,128)S(1)} async-done(((f32[32,1,864]{2,1,0:T(1,128)}), f32[32,1,864]{2,1,0:T(1,128)S(1)}, u32[]{:S(2)}, u32[]{:S(2)}) %all-to-all-start.1) | async-done | bytes 110624 | tf_op jit(solution)/shard_map/all_to_all | solution.py:117
  340.0 0.9 reduce.10
  341.6 1.4 copy.86
  343.0 1.9 reshape.1624
  345.0 4.0 convolution_bitcast_fusion
  348.9 7.3 %copy.87 = f32[384,12,144]{2,1,0:T(8,128)} copy(f32[384,12,144]{0,2,1:T(8,128)} %convolution_bitcast_fusion) | data formatting | bytes 5308416 | tf_op jit(solution)/shard_map/jk,pik->jip/transpose | solution.py:125
  356.3 6.6 %reshape.1625 = f32[4608,144]{1,0:T(8,128)} reshape(f32[384,12,144]{2,1,0:T(8,128)} %copy.87) | data formatting | bytes 5308416 | tf_op jit(solution)/shard_map/reshape | solution.py:127
  362.9 81.6 %reduce-scatter.2.cloned.1.call-done = f32[288,144]{1,0:T(8,128)} async-done(((f32[4608,144]{1,0:T(8,128)}), f32[288,144]{1,0:T(8,128)}) %reduce-scatter.2.cloned.1.call-update) | async-done | bytes 165904 | tf_op jit(solution)/shard_map/reduce_scatter | solution.py:126
  444.5 1.8 copy.88
  (478 shorter events, 195.7 us)
Async XLA Ops:
  6.5 295.2 %copy-start = (bf16[512,1024]{1,0:T(8,128)(2,1)S(1)}, bf16[512,1024]{1,0:T(8,128)(2,1)}, u32[]{:S(2)}) copy-start(bf16[512,1024]{1,0:T(8,128)(2,1)} %param.4) | copy-start | bytes 3145732
  305.0 15.2 %all-to-all-start = ((f32[32,1,576]{2,1,0:T(1,128)}), f32[32,1,576]{2,1,0:T(1,128)S(1)}, u32[]{:S(2)}, u32[]{:S(2)}) async-start(f32[32,1,576]{2,1,0:T(1,128)} %reshape.1773), calls=%async_computation | async-start | bytes 163840 | tf_op jit(solution)/shard_map/all_to_all | solution.py:114
  328.4 11.6 %all-to-all-start.1 = ((f32[32,1,864]{2,1,0:T(1,128)}), f32[32,1,864]{2,1,0:T(1,128)S(1)}, u32[]{:S(2)}, u32[]{:S(2)}) async-start(f32[32,1,864]{2,1,0:T(1,128)} %reshape.1775), calls=%async_computation.1 | async-start | bytes 229376 | tf_op jit(solution)/shard_map/all_to_all | solution.py:117
  333.9 110.6 %reduce-scatter.2.cloned.1.call-start = ((), (), s32[]{:S(2)}) async-start(), calls=%async_computation.3 | async-start | bytes 5013504 | tf_op jit(solution)/shard_map/reduce_scatter | solution.py:126
Sparse Core Ops, SparseCore 0:
  363.0 81.4 reduce-scatter.1
where the time goes:
time: 458 us; the launch traced here: 453 us
  other arithmetic  190 us (41%)
  waiting for transfers between devices  92 us (20%)
  loops' own time  83.5 us (18%)
  local copies, waits for them, and re-layouts  51.1 us (11%)
  starting transfers between devices  15.2 us (3%)
  between operations  13.7 us (3%)
  matrix products  7.21 us (2%)
    sqrt x128, other arithmetic, advance(): jnp.sqrt(jnp.maximum((2.0 * degree + 1.0) * (deg_sum - 1.0) * (deg_diff -...  84.1 us
    another operation x1, loops' own time, legendre_rows(): lax.scan(advance, start_pair, jnp.arange(degree_count, dtype=jnp.float32)...  83.5 us
    lt x128, other arithmetic, advance(): orders < degree  82.6 us
    reduce_scatter x1, waiting for transfers between devices, on_device(): lax.psum_scatter(grid_vals.reshape(pts_col * lax.axis_size('col'), pts_ro...  81.6 us
    gather x4, local copies, waits for them, and re-layouts, spectral_weights(): values = plm_table[:, degree * LL + orders]  10.9 us
    while x120, other arithmetic  10.2 us
    all_to_all x1, starting transfers between devices, on_device(): lax.all_to_all(second, 'row', split_axis=2, concat_axis=1, tiled=True)  9.41 us
  transfers between devices with their start and end apart: 3, of which 3 were waited for; matrix products, arithmetic and copies ran while one was open for 0% of the time, Pallas kernels for 0%

commit v1 on v0

v1 whole, which is shorter than its diff:
```python
import math

import jax
import jax.numpy as jnp
from jax import lax
from jax.experimental import pallas as pl
from jax.experimental.pallas import tpu as pltpu
from jax.sharding import PartitionSpec as P

LL = 128
NLON = 384
NLAT = 12
F32 = jnp.float32
BF16 = jnp.bfloat16
I32 = jnp.int32
MESH = pl.DeviceIdType.MESH

NROW = 32
NCOL = 16
ZW = 9
RW = 27
LANES = 384


def iota(shape, dim):
    return lax.broadcasted_iota(I32, shape, dim)


def split(x):
    hi = x.astype(BF16)
    return hi, (x - hi.astype(F32)).astype(BF16)


def mm(a, b, dims=((1,), (0,))):
    return lax.dot_general(a, b, (dims, ((), ())), preferred_element_type=F32)


def key_orders(pair, second, firsts):
    n = pair.shape[1]
    hit = iota((64, n), 0) == pair
    first = jnp.sum(jnp.where(hit, firsts, 0.0), axis=0, keepdims=True)
    other = jnp.where(first == 0.0, 64.0, 128.0 - first)
    return jnp.where(second == 0, first, other)


def fourier(j, m, parity):
    x = j * m + (NLON - (NLON // 4) * parity)
    p = x - NLON * jnp.floor(x * (1.0 / NLON))
    s = jnp.abs(p - NLON / 2) - NLON / 4
    t = s * (2.0 * math.pi / NLON)
    t2 = t * t
    r = -1.0 / 39916800.0
    for c in (1.0 / 362880.0, -1.0 / 5040.0, 1.0 / 120.0, -1.0 / 6.0, 1.0):
        r = r * t2 + c
    return r * t


def kernel(
    cov_hbm,
    coef_hbm,
    out,
    cov,
    coef,
    firsts,
    ta,
    tb,
    ts,
    tp,
    fz_hi,
    fz_lo,
    fr_hi,
    fr_lo,
    perm,
    c_send,
    c_recv,
    d_send,
    d_recv,
    a_send,
    a_recv,
    b_send,
    b_recv,
    oa,
    ob,
    oc,
    local_sem,
    ssem,
    rsem,
):
    r = lax.axis_index("row")
    c = lax.axis_index("col")
    zw = (ZW * c + NCOL - 1) // NCOL
    z_works = (NCOL * zw) // ZW == c
    rw = (RW * r + NROW - 1) // NROW
    r_works = (NROW * rw) // RW == r

    coef_copy = pltpu.make_async_copy(coef_hbm, coef, local_sem.at[0])
    coef_copy.start()
    cov_copy = pltpu.make_async_copy(cov_hbm, cov, local_sem.at[1])
    cov_copy.start()

    barrier = pltpu.get_barrier_semaphore()

    def greet_col(k, carry):
        pl.semaphore_signal(
            barrier, inc=1, device_id={"col": lax.rem(c + k, NCOL)}, device_id_type=MESH
        )
        return carry

    def greet_row(k, carry):
        pl.semaphore_signal(
            barrier, inc=1, device_id={"row": lax.rem(r + k, NROW)}, device_id_type=MESH
        )
        return carry

    lax.fori_loop(1, NCOL, greet_col, 0)
    lax.fori_loop(1, NROW, greet_row, 0)

    coef_copy.wait()
    for p in range(64):
        firsts[p : p + 1, :] = coef[1:2, 256 * p : 256 * p + 128].astype(F32)
    first_col = firsts[...][:, 0:1]

    lane = iota((1, LANES), 1)
    on_row = lane < 128
    y = lane - 128
    lat = jnp.where(on_row, lane // 8, y // 16)
    key = jnp.where(on_row, lane % 8, y % 16)
    pair = jnp.where(on_row, 2 * r, 4 * c) + key // 4
    m = key_orders(pair, (key // 2) % 2, first_col)
    delta = (lat.astype(F32) - 5.5) * (math.pi / 192)
    d2 = delta * delta
    cos_t = -delta * (1.0 - d2 * (1.0 / 6.0) * (1.0 - d2 * (1.0 / 20.0) * (1.0 - d2 * (1.0 / 42.0))))
    sin_t = 1.0 - d2 * 0.5 * (1.0 - d2 * (1.0 / 12.0) * (1.0 - d2 * (1.0 / 30.0)))
    deg = iota((LL, LANES), 0).astype(F32)
    diff = deg - m
    total = deg + m
    above = diff > 0.0
    inv = 1.0 / jnp.maximum(diff * total, 1.0)
    a = jnp.sqrt(jnp.maximum((2.0 * deg - 1.0) * (2.0 * deg + 1.0), 0.0) * inv)
    b = jnp.sqrt(
        jnp.maximum((2.0 * deg + 1.0) * (total - 1.0) * (diff - 1.0), 0.0)
        * inv
        / jnp.maximum(2.0 * deg - 3.0, 1.0)
    )
    ta[...] = jnp.where(above, a * cos_t, 0.0)
    tb[...] = jnp.where(above, b, 0.0)
    growth = jnp.sqrt((2.0 * deg + 1.0) / jnp.maximum(2.0 * deg, 1.0))
    growth = jnp.where(deg == 1.0, math.sqrt(3.0), growth)
    ts[...] = jnp.where(deg == 0.0, 1.0, growth * sin_t)

    def advance(block, state):
        before, earlier, sect = state
        base = pl.multiple_of(block * 8, 8)
        av, bv, sv = (t[pl.ds(base, 8), :] for t in (ta, tb, ts))
        rows = []
        for s in range(8):
            sect = sect * sv[s : s + 1]
            here = (block * 8 + s).astype(F32)
            now = jnp.where(m == here, sect, av[s : s + 1] * before - bv[s : s + 1] * earlier)
            rows.append(now)
            before, earlier = now, before
        tp[pl.ds(base, 8), :] = jnp.concatenate(rows, axis=0)
        return before, earlier, sect

    zero = jnp.zeros((1, LANES), F32)
    lax.fori_loop(0, LL // 8, advance, (zero, zero, zero + 1.0))

    table = tp[...].T
    keys = (2.0 * jnp.broadcast_to(m, (LL, LANES)) + (key % 2).astype(F32)).T[:, 0:1]

    def places(row, n, at):
        return coef[row : row + 1, pl.ds(pl.multiple_of(at, 512), n)]

    row_at, col_at = 512 * r, 1024 * c
    pick = jnp.where(iota((LL, 512), 0) == places(0, 512, row_at), 1.0, 0.0).astype(BF16)
    row_keys = (2 * places(1, 512, row_at) + places(2, 512, row_at)).astype(F32)
    w_row = mm(table[0:96].astype(BF16), pick)
    w_row = jnp.where(keys[0:96] == row_keys, w_row, 0.0).astype(BF16)

    pick = jnp.where(iota((LL, 1024), 0) == places(0, 1024, col_at), 1.0, 0.0).astype(BF16)
    col_keys = (2 * places(1, 1024, col_at) + places(2, 1024, col_at)).astype(F32)
    hit = keys[128:320] == col_keys
    t_hi, t_lo = split(table[128:320])
    w_hi = jnp.where(hit, mm(t_hi, pick), 0.0).astype(BF16)
    w_lo = jnp.where(hit, mm(t_lo, pick), 0.0).astype(BF16)

    cov_copy.wait()
    f_hi, f_lo = split(mm(w_row, cov[...]))
    last = ((1,), (1,))
    spec = mm(w_hi, f_hi, last) + mm(w_lo, f_hi, last) + mm(w_hi, f_lo, last)
    spec = jnp.concatenate([spec, jnp.zeros((192, 32), F32)], axis=1)

    turned = [spec] + [pltpu.roll(spec, 32 * k, 1) for k in (1, 2, 3)]
    quarter = iota((16, 128), 1) // 32
    for g in range(3):
        for t in range(3):
            tile = None
            for n in range(4):
                at = 16 * (4 * g + n)
                piece = turned[(n - t) % 4][at : at + 16]
                tile = piece if tile is None else jnp.where(quarter == n, piece, tile)
            c_send[3 * g + t] = tile

    pl.semaphore_wait(barrier, NCOL - 1 + NROW - 1)

    def c_copy(w, dst):
        return pltpu.make_async_remote_copy(
            c_send.at[w], c_recv.at[c], ssem.at[0], rsem.at[0], device_id={"col": dst}, device_id_type=MESH
        )

    def start_c(k, carry):
        w = lax.rem(zw + k, ZW)
        dst = (NCOL * w) // ZW

        @pl.when(dst != c)
        def _():
            c_copy(w, dst).start()

        return carry

    lax.fori_loop(0, ZW, start_c, 0)

    kappa = iota((1, 256), 1)
    order = key_orders(kappa // 4, (kappa // 2) % 2, first_col)
    parity = (kappa % 2).astype(F32)
    hi, lo = split(fourier(iota((NLON, 256), 0).astype(F32), order, parity))
    fz_hi[...] = hi
    fz_lo[...] = lo

    def synthesize(t_hi, t_lo, x):
        x_hi, x_lo = split(x)
        return mm(t_hi[...], x_hi) + mm(t_hi[...], x_lo) + mm(t_lo[...], x_hi)

    def d_copy(dst):
        return pltpu.make_async_remote_copy(
            d_send.at[dst], d_recv.at[zw], ssem.at[1], rsem.at[1], device_id={"col": dst}, device_id_type=MESH
        )

    @pl.when(z_works)
    def _():
        c_recv[c] = c_send[zw]
        pltpu.make_async_copy(c_recv.at[0 : NCOL - 1], c_recv.at[0 : NCOL - 1], rsem.at[0]).wait()
        got = synthesize(fz_hi, fz_lo, c_recv[...].reshape(256, 128))
        d_send[...] = got.reshape(NCOL, 24, 128)

        def start_d(k, carry):
            d_copy(lax.rem(c + k, NCOL)).start()
            return carry

        lax.fori_loop(1, NCOL, start_d, 0)
        d_recv[zw] = d_send[c]

    place = iota((512, 1), 0)
    lon = 12 * (place // 16) + place % 16
    hi, lo = split(fourier(lon.astype(F32), order, parity))
    fr_hi[...] = hi
    fr_lo[...] = lo

    @pl.when(z_works)
    def _():
        pltpu.make_async_copy(d_recv.at[0 : ZW - 1], d_recv.at[0 : ZW - 1], rsem.at[1]).wait()

    @pl.when(jnp.logical_not(z_works))
    def _():
        pltpu.make_async_copy(d_recv, d_recv, rsem.at[1]).wait()

    x = d_recv[...].reshape(24 * ZW, 128)
    sub, ln = iota((24 * ZW, 128), 0), iota((24 * ZW, 128), 1)
    for s in (1, 2, 4):
        sbit, lbit = (sub & s) != 0, (ln & s) != 0
        down = pltpu.roll(pltpu.roll(x, s, 0), 128 - s, 1)
        up = pltpu.roll(pltpu.roll(x, 24 * ZW - s, 0), s, 1)
        x = jnp.where(sbit == lbit, x, jnp.where(sbit, down, up))
    a_send[...] = x.reshape(RW, 8, 128)

    def a_copy(v, dst):
        return pltpu.make_async_remote_copy(
            a_send.at[v], a_recv.at[r], ssem.at[2], rsem.at[2], device_id={"row": dst}, device_id_type=MESH
        )

    def start_a(k, carry):
        v = lax.rem(rw + k, RW)
        dst = (NROW * v) // RW

        @pl.when(dst != r)
        def _():
            a_copy(v, dst).start()

        return carry

    lax.fori_loop(0, RW, start_a, 0)

    for g in range(3):
        u, v = iota((128, 512), 0), iota((128, 512), 1)
        goes = 128 * ((u // 8) % 4) + 12 * (u % 8) + 4 * g + u // 32
        perm[128 * g : 128 * g + 128] = jnp.where(goes == v, 1.0, 0.0).astype(BF16)

    def b_copy(dst):
        return pltpu.make_async_remote_copy(
            b_send.at[dst], b_recv.at[rw], ssem.at[3], rsem.at[3], device_id={"row": dst}, device_id_type=MESH
        )

    @pl.when(r_works)
    def _():
        a_recv[r] = a_send[rw]
        pltpu.make_async_copy(a_recv.at[0 : NROW - 1], a_recv.at[0 : NROW - 1], rsem.at[2]).wait()
        got = synthesize(fr_hi, fr_lo, a_recv[...].reshape(256, 128))
        b_send[...] = got.reshape(NROW, 16, 128)

        def start_b(k, carry):
            b_copy(lax.rem(r + k, NROW)).start()
            return carry

        lax.fori_loop(1, NROW, start_b, 0)
        b_recv[rw] = b_send[r]
        pltpu.make_async_copy(b_recv.at[0 : RW - 1], b_recv.at[0 : RW - 1], rsem.at[3]).wait()

    @pl.when(jnp.logical_not(r_works))
    def _():
        pltpu.make_async_copy(b_recv, b_recv, rsem.at[3]).wait()

    x_hi, x_lo = split(b_recv[...].reshape(3, 144, 128))
    grid = None
    for g in range(3):
        p_g = perm[128 * g : 128 * g + 128]
        part = mm(x_hi[g], p_g) + mm(x_lo[g], p_g)
        grid = part if grid is None else grid + part
    ln = iota((16, 128), 1)
    for t in range(3):
        for n in range(4):
            z0, z1, z2 = (
                grid[48 * t + 16 * k : 48 * t + 16 * k + 16, 128 * n : 128 * n + 128] for k in range(3)
            )
            z1, z2 = pltpu.roll(z1, 96, 1), pltpu.roll(z2, 64, 1)
            o0 = jnp.where(ln < 96, z0, z1)
            o1 = jnp.where(ln < 64, z1, z2)
            rows = pl.ds(4 * t + n, 12, stride=12)
            oa[rows, :] = o0[0:12]
            ob[rows, :] = o1[0:12]
            oc[rows, :] = z2[0:12]
    out[:, 0:128] = oa[...]
    out[:, 128:256] = ob[...]
    out[:, 256:288] = oc[...][:, 0:32]

    @pl.when(z_works)
    def _():
        pltpu.make_async_copy(c_send.at[0 : ZW - 1], c_send.at[0 : ZW - 1], ssem.at[0]).wait()
        pltpu.make_async_copy(d_send.at[0 : NCOL - 1], d_send.at[0 : NCOL - 1], ssem.at[1]).wait()

    @pl.when(jnp.logical_not(z_works))
    def _():
        pltpu.make_async_copy(c_send, c_send, ssem.at[0]).wait()

    @pl.when(r_works)
    def _():
        pltpu.make_async_copy(a_send.at[0 : RW - 1], a_send.at[0 : RW - 1], ssem.at[2]).wait()
        pltpu.make_async_copy(b_send.at[0 : NROW - 1], b_send.at[0 : NROW - 1], ssem.at[3]).wait()

    @pl.when(jnp.logical_not(r_works))
    def _():
        pltpu.make_async_copy(a_send, a_send, ssem.at[2]).wait()


def on_device(covariance, coef_index):
    v = pltpu.VMEM
    return pl.pallas_call(
        kernel,
        out_shape=jax.ShapeDtypeStruct((144, 288), F32),
        in_specs=[pl.BlockSpec(memory_space=pl.ANY)] * 2,
        out_specs=pl.BlockSpec(memory_space=pltpu.VMEM),
        scratch_shapes=[
            v((512, 1024), BF16),
            v((3, 16384), I32),
            v((64, 128), F32),
            v((LL, LANES), F32),
            v((LL, LANES), F32),
            v((LL, LANES), F32),
            v((LL, LANES), F32),
            v((NLON, 256), BF16),
            v((NLON, 256), BF16),
            v((512, 256), BF16),
            v((512, 256), BF16),
            v((384, 512), BF16),
            v((ZW, 16, 128), F32),
            v((NCOL, 16, 128), F32),
            v((NCOL, 24, 128), F32),
            v((ZW, 24, 128), F32),
            v((RW, 8, 128), F32),
            v((NROW, 8, 128), F32),
            v((NROW, 16, 128), F32),
            v((RW, 16, 128), F32),
            v((144, 128), F32),
            v((144, 128), F32),
            v((144, 128), F32),
            pltpu.SemaphoreType.DMA((2,)),
            pltpu.SemaphoreType.DMA((4,)),
            pltpu.SemaphoreType.DMA((4,)),
        ],
        compiler_params=pltpu.CompilerParams(collective_id=0, has_side_effects=True),
    )(covariance, coef_index)


def solution(mesh):
    return jax.shard_map(
        on_device,
        mesh=mesh,
        in_specs=(P("row", "col"), P()),
        out_specs=P("row", "col"),
        check_vma=False,
    )
```

time: 458 us -> 50.8 us (0.11)
  the two profiles are of different devices: /device:TPU:6 before, /device:TPU:1 now
where the time goes in v1:
time: 50.8 us; the launch traced here: 50.6 us
  Pallas kernels  49 us (96%)
  local copies, waits for them, and re-layouts  1.64 us (3%)
    pallas_call x1, Pallas kernels, on_device(): pl.pallas_call(kernel, out_shape=jax.ShapeDtypeStruct((144, 288), F32), i...  49 us
    unnamed x1, local copies, waits for them, and re-layouts  1.64 us

profile of v1, /device:TPU:1, one launch (start us, length us, event | category | flops | bytes accessed | tf_op | source)
XLA Modules:
  0.0 50.6 jit_solution(8756448799687161660)
XLA Ops:
  0.0 49.0 %shard_map.28 = f32[144,288]{1,0:T(8,128)} custom-call(bf16[512,1024]{1,0:T(8,128)(2,1)} %cov_hbm.1, s32[3,16384]{1,0:T(4,128)} %coef_hbm.1), custom_call_target="tpu_custom_call" | custom-call | tf_op jit(solution)/shard_map/pallas_call | solution.py:366
  49.0 1.6 %copy.4 = f32[144,288]{1,0:T(8,128)} copy(f32[144,288]{1,0:T(8,128)} %shard_map.28) | data formatting | bytes 331776

commit v2 on v1

--- a/solution.py
+++ b/solution.py
@@ -19,6 +19,7 @@
 NCOL = 16
 ZW = 9
 RW = 27
+ZONE = 13
 LANES = 384
 
 
@@ -53,6 +54,31 @@
     for c in (1.0 / 362880.0, -1.0 / 5040.0, 1.0 / 120.0, -1.0 / 6.0, 1.0):
         r = r * t2 + c
     return r * t
+
+
+def col_worker(z):
+    w = jnp.where(z >= ZONE, z - ZONE, z + (NCOL - ZONE))
+    return w, w < ZW
+
+
+def row_worker(y):
+    return y, y < RW
+
+
+def ring(a, b):
+    return min((a - b) % 4, (b - a) % 4)
+
+
+COL_STEPS = sorted(range(1, NCOL), key=lambda k: -min(k, NCOL - k))
+D_ORDER = (4, 3, 2, 1, 0, 5, 6, 7, 15, 14, 8, 13, 9, 12, 10, 11)
+ROW_STEPS = sorted(
+    [(dy, dx, dc) for dy in range(4) for dx in range(4) for dc in range(2) if dy or dx or dc],
+    key=lambda k: -(3 * ring(k[0], 0) + 3 * ring(k[1], 0) + k[2]),
+)
+
+
+def wrap(x, n):
+    return jnp.where(x >= n, x - n, x)
 
 
 def kernel(
@@ -88,32 +114,44 @@
 ):
     r = lax.axis_index("row")
     c = lax.axis_index("col")
-    zw = (ZW * c + NCOL - 1) // NCOL
-    z_works = (NCOL * zw) // ZW == c
-    rw = (RW * r + NROW - 1) // NROW
-    r_works = (NROW * rw) // RW == r
+    zw, z_works = col_worker(c)
+    rw, r_works = row_worker(r)
+    core = lax.rem(r, 2)
+    at_x, at_y = lax.rem(lax.div(r, 2), 4), lax.div(r, 8)
+    ys, xs = [8 * wrap(at_y + k, 4) for k in range(4)], [2 * wrap(at_x + k, 4) for k in range(4)]
+    cores = [core, 1 - core]
+
+    def row_step(step):
+        dy, dx, dc = step
+        return ys[dy] + xs[dx] + cores[dc]
+
 
     coef_copy = pltpu.make_async_copy(coef_hbm, coef, local_sem.at[0])
     coef_copy.start()
     cov_copy = pltpu.make_async_copy(cov_hbm, cov, local_sem.at[1])
     cov_copy.start()
 
+    b_recv[...] = jnp.zeros((RW, 16, 128), F32)
     barrier = pltpu.get_barrier_semaphore()
 
     def greet_col(k, carry):
-        pl.semaphore_signal(
-            barrier, inc=1, device_id={"col": lax.rem(c + k, NCOL)}, device_id_type=MESH
+        dst = wrap(c + k, NCOL)
+
+        @pl.when(jnp.logical_or(z_works, col_worker(dst)[1]))
+        def _():
+            pl.semaphore_signal(barrier, inc=1, device_id={"col": dst}, device_id_type=MESH)
+
+        return carry
+
+    for step in ROW_STEPS:
+        to_row = row_step(step)
+        needs = jnp.logical_or(r_works, row_worker(to_row)[1])
+        pl.when(needs)(
+            lambda to_row=to_row: pl.semaphore_signal(
+                barrier, inc=1, device_id={"row": to_row}, device_id_type=MESH
+            )
         )
-        return carry
-
-    def greet_row(k, carry):
-        pl.semaphore_signal(
-            barrier, inc=1, device_id={"row": lax.rem(r + k, NROW)}, device_id_type=MESH
-        )
-        return carry
-
     lax.fori_loop(1, NCOL, greet_col, 0)
-    lax.fori_loop(1, NROW, greet_row, 0)
 
     coef_copy.wait()
     for p in range(64):
@@ -201,24 +239,17 @@
                 tile = piece if tile is None else jnp.where(quarter == n, piece, tile)
             c_send[3 * g + t] = tile
 
-    pl.semaphore_wait(barrier, NCOL - 1 + NROW - 1)
+    pl.semaphore_wait(barrier, jnp.where(z_works, NCOL - 1, ZW) + jnp.where(r_works, NROW - 1, RW))
 
     def c_copy(w, dst):
         return pltpu.make_async_remote_copy(
             c_send.at[w], c_recv.at[c], ssem.at[0], rsem.at[0], device_id={"col": dst}, device_id_type=MESH
         )
 
-    def start_c(k, carry):
-        w = lax.rem(zw + k, ZW)
-        dst = (NCOL * w) // ZW
-
-        @pl.when(dst != c)
-        def _():
-            c_copy(w, dst).start()
-
-        return carry
-
-    lax.fori_loop(0, ZW, start_c, 0)
+    for step in COL_STEPS:
+        to_col = wrap(c + step, NCOL)
+        w, works = col_worker(to_col)
+        pl.when(works)(lambda w=w, to_col=to_col: c_copy(w, to_col).start())
 
     kappa = iota((1, 256), 1)
     order = key_orders(kappa // 4, (kappa // 2) % 2, first_col)
@@ -243,11 +274,8 @@
         got = synthesize(fz_hi, fz_lo, c_recv[...].reshape(256, 128))
         d_send[...] = got.reshape(NCOL, 24, 128)
 
-        def start_d(k, carry):
-            d_copy(lax.rem(c + k, NCOL)).start()
-            return carry
-
-        lax.fori_loop(1, NCOL, start_d, 0)
+        for dst in D_ORDER:
+            pl.when(c != dst)(lambda dst=dst: d_copy(dst).start())
         d_recv[zw] = d_send[c]
 
     place = iota((512, 1), 0)
@@ -278,17 +306,10 @@
             a_send.at[v], a_recv.at[r], ssem.at[2], rsem.at[2], device_id={"row": dst}, device_id_type=MESH
         )
 
-    def start_a(k, carry):
-        v = lax.rem(rw + k, RW)
-        dst = (NROW * v) // RW
-
-        @pl.when(dst != r)
-        def _():
-            a_copy(v, dst).start()
-
-        return carry
-
-    lax.fori_loop(0, RW, start_a, 0)
+    for step in ROW_STEPS:
+        to_row = row_step(step)
+        v, works = row_worker(to_row)
+        pl.when(works)(lambda v=v, to_row=to_row: a_copy(v, to_row).start())
 
     for g in range(3):
         u, v = iota((128, 512), 0), iota((128, 512), 1)
@@ -297,7 +318,7 @@
 
     def b_copy(dst):
         return pltpu.make_async_remote_copy(
-            b_send.at[dst], b_recv.at[rw], ssem.at[3], rsem.at[3], device_id={"row": dst}, device_id_type=MESH
+            b_send.at[dst, 0:12], b_recv.at[rw, 0:12], ssem.at[3], rsem.at[3], device_id={"row": dst}, device_id_type=MESH
         )
 
     @pl.when(r_works)
@@ -307,17 +328,14 @@
         got = synthesize(fr_hi, fr_lo, a_recv[...].reshape(256, 128))
         b_send[...] = got.reshape(NROW, 16, 128)
 
-        def start_b(k, carry):
-            b_copy(lax.rem(r + k, NROW)).start()
-            return carry
-
-        lax.fori_loop(1, NROW, start_b, 0)
+        for step in ROW_STEPS:
+            b_copy(row_step(step)).start()
         b_recv[rw] = b_send[r]
-        pltpu.make_async_copy(b_recv.at[0 : RW - 1], b_recv.at[0 : RW - 1], rsem.at[3]).wait()
+        pltpu.make_async_copy(b_recv.at[0 : RW - 1, 0:12], b_recv.at[0 : RW - 1, 0:12], rsem.at[3]).wait()
 
     @pl.when(jnp.logical_not(r_works))
     def _():
-        pltpu.make_async_copy(b_recv, b_recv, rsem.at[3]).wait()
+        pltpu.make_async_copy(b_recv.at[:, 0:12], b_recv.at[:, 0:12], rsem.at[3]).wait()
 
     x_hi, x_lo = split(b_recv[...].reshape(3, 144, 128))
     grid = None
@@ -354,7 +372,7 @@
     @pl.when(r_works)
     def _():
         pltpu.make_async_copy(a_send.at[0 : RW - 1], a_send.at[0 : RW - 1], ssem.at[2]).wait()
-        pltpu.make_async_copy(b_send.at[0 : NROW - 1], b_send.at[0 : NROW - 1], ssem.at[3]).wait()
+        pltpu.make_async_copy(b_send.at[0 : NROW - 1, 0:12], b_send.at[0 : NROW - 1, 0:12], ssem.at[3]).wait()
 
     @pl.when(jnp.logical_not(r_works))
     def _():
@@ -365,7 +383,7 @@
     v = pltpu.VMEM
     return pl.pallas_call(
         kernel,
-        out_shape=jax.ShapeDtypeStruct((144, 288), F32),
+        out_shape=pltpu.VMEM((144, 288), F32),
         in_specs=[pl.BlockSpec(memory_space=pl.ANY)] * 2,
         out_specs=pl.BlockSpec(memory_space=pltpu.VMEM),
         scratch_shapes=[

time: 50.8 us -> 44.6 us (0.88)
  Pallas kernels: 49 us -> 43.8 us
  local copies, waits for them, and re-layouts: 1.64 us -> 0.69 us
    pallas_call x1, Pallas kernels: 49 us -> 43.8 us  [on_device(): pl.pallas_call(kernel, out_shape=pltpu.VMEM((144, 288), F32), in_specs=[p...]
    unnamed x1, local copies, waits for them, and re-layouts: 1.64 us -> 0.69 us
where the time goes in v2:
time: 44.6 us; the launch traced here: 44.5 us
  Pallas kernels  43.8 us (98%)
  local copies, waits for them, and re-layouts  0.69 us (2%)
    pallas_call x1, Pallas kernels, on_device(): pl.pallas_call(kernel, out_shape=pltpu.VMEM((144, 288), F32), in_specs=[p...  43.8 us

profile of v2, /device:TPU:1, one launch (start us, length us, event | category | flops | bytes accessed | tf_op | source)
XLA Modules:
  0.0 44.5 jit_solution(9077125599492958340)
XLA Ops:
  0.0 43.8 %shard_map.28 = f32[144,288]{1,0:T(8,128)S(1)} custom-call(bf16[512,1024]{1,0:T(8,128)(2,1)} %cov_hbm.1, s32[3,16384]{1,0:T(4,128)} %coef_hbm.1), custom_call_target="tpu_custom_call" | custom-call | tf_op jit(solution)/shard_map/pallas_call | solution.py:384
  43.8 0.7 %copy.4 = f32[144,288]{1,0:T(8,128)} copy(f32[144,288]{1,0:T(8,128)S(1)} %shard_map.28) | data formatting | bytes 331776

commit v3 on v2

--- a/solution.py
+++ b/solution.py
@@ -19,7 +19,7 @@
 NCOL = 16
 ZW = 9
 RW = 27
-ZONE = 13
+WORKERS = (0, 1, 15, 3, 13, 4, 12, 6, 7)
 LANES = 384
 
 
@@ -57,8 +57,10 @@
 
 
 def col_worker(z):
-    w = jnp.where(z >= ZONE, z - ZONE, z + (NCOL - ZONE))
-    return w, w < ZW
+    w, works = 0, False
+    for k, at in enumerate(WORKERS):
+        w, works = jnp.where(z == at, k, w), jnp.logical_or(works, z == at)
+    return w, works
 
 
 def row_worker(y):
@@ -70,7 +72,7 @@
 
 
 COL_STEPS = sorted(range(1, NCOL), key=lambda k: -min(k, NCOL - k))
-D_ORDER = (4, 3, 2, 1, 0, 5, 6, 7, 15, 14, 8, 13, 9, 12, 10, 11)
+D_ORDER = (0, 1, 2, 3, 4, 5, 6, 7, 15, 14, 13, 8, 12, 9, 10, 11)
 ROW_STEPS = sorted(
     [(dy, dx, dc) for dy in range(4) for dx in range(4) for dc in range(2) if dy or dx or dc],
     key=lambda k: -(3 * ring(k[0], 0) + 3 * ring(k[1], 0) + k[2]),
@@ -134,15 +136,6 @@
     b_recv[...] = jnp.zeros((RW, 16, 128), F32)
     barrier = pltpu.get_barrier_semaphore()
 
-    def greet_col(k, carry):
-        dst = wrap(c + k, NCOL)
-
-        @pl.when(jnp.logical_or(z_works, col_worker(dst)[1]))
-        def _():
-            pl.semaphore_signal(barrier, inc=1, device_id={"col": dst}, device_id_type=MESH)
-
-        return carry
-
     for step in ROW_STEPS:
         to_row = row_step(step)
         needs = jnp.logical_or(r_works, row_worker(to_row)[1])
@@ -151,7 +144,11 @@
                 barrier, inc=1, device_id={"row": to_row}, device_id_type=MESH
             )
         )
-    lax.fori_loop(1, NCOL, greet_col, 0)
+    for z in range(NCOL):
+        needs = c != z if z in WORKERS else z_works
+        pl.when(needs)(
+            lambda z=z: pl.semaphore_signal(barrier, inc=1, device_id={"col": z}, device_id_type=MESH)
+        )
 
     coef_copy.wait()
     for p in range(64):

time: 44.6 us -> 42.4 us (0.951)
  Pallas kernels: 43.8 us -> 41.6 us
    pallas_call x1, Pallas kernels: 43.8 us -> 41.6 us  [on_device(): pl.pallas_call(kernel, out_shape=pltpu.VMEM((144, 288), F32), in_specs=[p...]
where the time goes in v3:
time: 42.4 us; the launch traced here: 42.3 us
  Pallas kernels  41.6 us (98%)
  local copies, waits for them, and re-layouts  0.69 us (2%)
    pallas_call x1, Pallas kernels, on_device(): pl.pallas_call(kernel, out_shape=pltpu.VMEM((144, 288), F32), in_specs=[p...  41.6 us

profile of v3, /device:TPU:1, one launch (start us, length us, event | category | flops | bytes accessed | tf_op | source)
XLA Modules:
  0.0 42.3 jit_solution(14358131338945945564)
XLA Ops:
  0.0 41.6 %shard_map.28 = f32[144,288]{1,0:T(8,128)S(1)} custom-call(bf16[512,1024]{1,0:T(8,128)(2,1)} %cov_hbm.1, s32[3,16384]{1,0:T(4,128)} %coef_hbm.1), custom_call_target="tpu_custom_call" | custom-call | tf_op jit(solution)/shard_map/pallas_call | solution.py:381
  41.6 0.7 %copy.4 = f32[144,288]{1,0:T(8,128)} copy(f32[144,288]{1,0:T(8,128)S(1)} %shard_map.28) | data formatting | bytes 331776

commit v4 on v3

--- a/solution.py
+++ b/solution.py
@@ -271,7 +271,7 @@
         got = synthesize(fz_hi, fz_lo, c_recv[...].reshape(256, 128))
         d_send[...] = got.reshape(NCOL, 24, 128)
 
-        for dst in D_ORDER:
+        for dst in D_ORDER[:8]:
             pl.when(c != dst)(lambda dst=dst: d_copy(dst).start())
         d_recv[zw] = d_send[c]
 
@@ -280,6 +280,11 @@
     hi, lo = split(fourier(lon.astype(F32), order, parity))
     fr_hi[...] = hi
     fr_lo[...] = lo
+
+    @pl.when(z_works)
+    def _():
+        for dst in D_ORDER[8:]:
+            pl.when(c != dst)(lambda dst=dst: d_copy(dst).start())
 
     @pl.when(z_works)
     def _():

time: 42.4 us -> 42.6 us (level)
  no operation moved by 1% of the time
where the time goes in v4:
time: 42.6 us; the launch traced here: 42.4 us
  Pallas kernels  41.7 us (98%)
  local copies, waits for them, and re-layouts  0.69 us (2%)
    pallas_call x1, Pallas kernels, on_device(): pl.pallas_call(kernel, out_shape=pltpu.VMEM((144, 288), F32), in_specs=[p...  41.7 us

profile of v4, /device:TPU:1, one launch (start us, length us, event | category | flops | bytes accessed | tf_op | source)
XLA Modules:
  0.0 42.4 jit_solution(9594442123030962865)
XLA Ops:
  0.0 41.7 %shard_map.28 = f32[144,288]{1,0:T(8,128)S(1)} custom-call(bf16[512,1024]{1,0:T(8,128)(2,1)} %cov_hbm.1, s32[3,16384]{1,0:T(4,128)} %coef_hbm.1), custom_call_target="tpu_custom_call" | custom-call | tf_op jit(solution)/shard_map/pallas_call | solution.py:386
  41.7 0.7 %copy.4 = f32[144,288]{1,0:T(8,128)} copy(f32[144,288]{1,0:T(8,128)S(1)} %shard_map.28) | data formatting | bytes 331776
